TPU v7x, 32 devices: a whole 2x2x4 slice. The times are simulated.
32 devices in a mesh: groups: 2 (over x), seq: 16 (over z, y, core).
Axes of the slice: x: 2, y: 2, z: 4, core: 2. Of those that a mesh axis runs over, the one named last changes fastest.
Arguments:
- enc_input: bfloat16 [8192, 1408], P(('groups', 'seq')), parts along dimension 0, may hold values from -6 to 6
- enc_weight: bfloat16 [2816, 1536], P('seq'), may hold values from -0.109375 to 0.109375
- norm_gain: float32 [1536], replicated, may hold values from 0.5 to 1.5
- q_weight: bfloat16 [1536, 1024], replicated, may hold values from -1 to 1
- kv_weight: bfloat16 [1536, 320], replicated, may hold values from -1 to 1
- out_weight: bfloat16 [1536, 1536], replicated, may hold values from -0.15625 to 0.15625
- dec_weight: float32 [3, 1536], replicated, may hold values from -3 to 3
- track_weight: bfloat16 [192, 1536], P('seq'), may hold values from -0.15625 to 0.15625
- track_grad: bfloat16 [4096, 192], P('groups', 'seq'), parts along dimension 0, may hold values from -6 to 6
- track_index: int32 [384], P('groups'), parts along dimension 0, may hold values from 0 to 191, each once
- track_mask: int32 [384], P('groups'), parts along dimension 0, may hold values 0 or 1
Outputs:
- trunk_out: bfloat16 [4096, 1536], P(('groups', 'seq')), parts along dimension 0
- skip_grad: bfloat16 [4096, 1536], P(('groups', 'seq')), parts along dimension 0
- dec_weight_grad: float32 [6, 1536], P('groups'), parts along dimension 0
There are 2 independent parts, one for each index of `groups`. A program takes and returns all parts, laid end to end along the dimension named above; an argument that names none is the same for every part. Nothing has to cross between parts.
Inputs may be any that keep to these rules, and one draw needn't show every extreme that they name: `track_index`: names every track once.
All inputs are finite; a program needn't handle non-finite values.
Results may differ from a plain program's by a relative error of at most 0.02.
Values may be sent and summed in bfloat16 or wider, within the bound.
No kernel may reach another device: no remote copies, remote signals or barrier semaphores. Data moves between devices by JAX's collectives and lax.ppermute only.
A program may use at most 128 MiB of HBM per device.

v0:
```python
import math
import jax
import jax.numpy as jnp
from jax import lax
from jax.sharding import PartitionSpec as P

HEADS = 8
QK = 128
VDIM = 192
DILATION_SPAN = 8


def with_halo(cells, sides, width):
    for axis, dim in sides:
        count = lax.axis_size(axis)
        ends = count - 1
        head = lax.slice_in_dim(cells, 0, width, axis=dim)
        tail = lax.slice_in_dim(cells, cells.shape[dim] - width, cells.shape[dim], axis=dim)
        cells = jnp.concatenate(
            [
                lax.ppermute(tail, axis, [(i, (i + 1) % count) for i in range(ends)]),
                cells,
                lax.ppermute(head, axis, [((i + 1) % count, i) for i in range(ends)]),
            ],
            axis=dim,
        )
    return cells


def gelu_tanh(values):
    return jax.nn.gelu(values, approximate=True)


def attention(tokens, tok_f, norm_gain, q_weight, kv_weight, out_weight):
    token_rows = tokens.shape[0]
    normed = (
        tok_f * lax.rsqrt(jnp.mean(tok_f * tok_f, axis=-1, keepdims=True) + 1e-06) * norm_gain
    ).astype(jnp.bfloat16)
    query = jnp.dot(normed, q_weight, preferred_element_type=jnp.float32).astype(jnp.bfloat16)
    keyval = jnp.dot(normed, kv_weight, preferred_element_type=jnp.float32).astype(jnp.bfloat16)
    query_rows = query.reshape(token_rows * HEADS, QK)

    def block_update(carry, key_block):
        running_max, running_sum, weighted = carry
        scores = lax.dot_general(
            query_rows,
            key_block[:, :QK],
            (((1,), (1,)), ((), ())),
            preferred_element_type=jnp.float32,
        ) * QK ** (-0.5)
        new_max = jnp.maximum(running_max, jnp.max(scores, axis=1))
        shrink = jnp.exp(running_max - new_max)
        expw = jnp.exp(scores - new_max[:, None])
        running_sum = running_sum * shrink + jnp.sum(expw, axis=1)
        weighted = weighted * shrink[:, None] + jnp.dot(
            expw.astype(jnp.bfloat16), key_block[:, QK:], preferred_element_type=jnp.float32
        )
        return (new_max, running_sum, weighted)

    start_state = (
        jnp.full((token_rows * HEADS,), -1e30, jnp.float32),
        jnp.zeros((token_rows * HEADS,), jnp.float32),
        jnp.zeros((token_rows * HEADS, VDIM), jnp.float32),
    )
    carry = start_state
    piece = lax.all_gather(keyval, "seq", axis=0, tiled=True)
    count = piece.shape[0]

    def step_fn(inner, key_block):
        return (block_update(inner, key_block), 0)

    carry, unused = lax.scan(step_fn, carry, piece.reshape(count // 128, 128, piece.shape[1]))
    running_max, running_sum, weighted = carry
    context = (
        (weighted / running_sum[:, None]).reshape(token_rows, HEADS * VDIM).astype(jnp.bfloat16)
    )
    return (tok_f + jnp.dot(context, out_weight, preferred_element_type=jnp.float32)).astype(
        jnp.bfloat16
    )


def decoder_back(tok_f, dec_weight, track_weight, track_grad, track_index, track_mask):
    token_rows = tok_f.shape[0]
    exchanged = lax.all_to_all(track_grad, "seq", split_axis=0, concat_axis=1, tiled=True)
    masked = exchanged * track_mask.astype(jnp.bfloat16)[None, :]
    every_row = lax.all_gather(track_weight, "seq", axis=0, tiled=True)
    selected = jnp.take(every_row, track_index, axis=0)
    head_f = jnp.dot(masked, selected, preferred_element_type=jnp.float32)
    head_gradient = head_f.astype(jnp.bfloat16)
    padded_input = with_halo(head_gradient, (("seq", 0),), DILATION_SPAN).astype(jnp.float32)
    skip_act, pullback = jax.vjp(gelu_tanh, tok_f)
    convback = jnp.zeros(tok_f.shape, jnp.float32)
    tap_terms = []
    for shift_amount in range(3):
        shifted_rows = padded_input[
            DILATION_SPAN * (2 - shift_amount) : DILATION_SPAN * (2 - shift_amount) + token_rows
        ]
        convback = convback + dec_weight[shift_amount][None, :] * shifted_rows
        tap_terms.append(jnp.sum(skip_act * shifted_rows, axis=0))
    skip_grad = pullback(convback)[0].astype(jnp.bfloat16)
    summed = lax.psum(jnp.stack(tap_terms, axis=0), "seq")
    dec_weight_grad = summed / jnp.float32(math.sqrt(token_rows * lax.axis_size("seq")))
    return (skip_grad, dec_weight_grad)


def shards(
    enc_input,
    enc_weight,
    norm_gain,
    q_weight,
    kv_weight,
    out_weight,
    dec_weight,
    track_weight,
    track_grad,
    track_index,
    track_mask,
):
    token_rows = enc_input.shape[0] // 2
    patches = enc_input.reshape(token_rows, 2 * enc_input.shape[1])
    tok_sum = jnp.dot(
        patches,
        lax.all_gather(enc_weight, "seq", axis=0, tiled=True),
        preferred_element_type=jnp.float32,
    )
    tokens = tok_sum.astype(jnp.bfloat16)
    tok_f = tokens.astype(jnp.float32)
    trunk_out = attention(tokens, tok_f, norm_gain, q_weight, kv_weight, out_weight)
    skip_grad, dec_weight_grad = decoder_back(
        tok_f, dec_weight, track_weight, track_grad, track_index, track_mask
    )
    return (trunk_out, skip_grad, dec_weight_grad)


def solution(mesh):
    return jax.shard_map(
        shards,
        mesh=mesh,
        in_specs=(
            P(("groups", "seq"), None),
            P("seq", None),
            P(),
            P(),
            P(),
            P(),
            P(),
            P("seq", None),
            P("groups", "seq"),
            P("groups"),
            P("groups"),
        ),
        out_specs=(P(("groups", "seq"), None), P(("groups", "seq"), None), P("groups", None)),
        check_vma=False,
    )
```

profile of v0, /device:TPU:0, one launch (start us, length us, event | category | flops | bytes accessed | tf_op | source)
XLA Modules:
  0.0 272.7 jit_solution(8789962556055584525)
XLA Ops:
  9.6 7.4 %all-to-all-start = ((bf16[16,128,12]{1,2,0:T(8,128)(2,1)}), bf16[16,128,12]{1,2,0:T(8,128)(2,1)S(1)}, u32[]{:S(2)}, u32[]{:S(2)}) async-start(bf16[16,128,12]{1,2,0:T(8,128)(2,1)} %copy.20), calls=%async_computation | async-start | bytes 131072 | tf_op jit(solution)/shard_map/all_to_all | solution.py:84
  17.1 30.1 %all-gather = bf16[16,12,1536]{2,1,0:T(8,128)(2,1)} all-gather(bf16[1,12,1536]{2,1,0:T(8,128)(2,1)} %bitcast.28), channel_id=1, replica_groups=mesh['groups'=2,'seq'=16] {'seq'}, dimensions={0}, use_global_device_ids=true | all-gather | bytes 626688 | tf_op jit(solution)/shard_map/all_gather | solution.py:86
  51.3 3.6 %gather_fusion = bf16[192,1536]{1,0:T(8,128)(2,1)} fusion(bf16[192,1536]{1,0:T(8,128)(2,1)} %reshape.51, s32[1024]{0:T(1024)S(1)} %pad_clamp_fusion), kind=kCustom, calls=%fused_computation | custom fusion | bytes 1180416 | tf_op jit(solution)/shard_map/jit(_take)/gather | solution.py:87
  57.7 2.8 %collective-permute-start = (bf16[8,1536]{1,0:T(8,128)(2,1)}, bf16[8,1536]{1,0:T(8,128)(2,1)}, u32[]{:S(2)}, u32[]{:S(2)}) collective-permute-start(bf16[8,1536]{1,0:T(8,128)(2,1)} %get-tuple-element.101), channel_id=1, source_target_pairs={{0,1},{1,2},{2,3},{3,4},{4,5},{5,6},{6,7},{7,8},{8,9},{9,10},{10,1... | collective-permute-start | bytes 73736 | tf_op jit(solution)/shard_map/ppermute | solution.py:21
  67.2 26.1 %all-gather.4.cloned.1.call-done = bf16[2816,1536]{1,0:T(8,128)(2,1)} async-done(((bf16[176,1536]{1,0:T(8,128)(2,1)}), bf16[2816,1536]{1,0:T(8,128)(2,1)}) %all-gather.4.cloned.1.call-update) | async-done | bytes 8650768 | tf_op jit(solution)/shard_map/all_gather | solution.py:123
  93.3 7.5 %multiply_reduce_fusion.3 = (f32[1536]{0:T(1024)S(1)}, f32[1536]{0:T(1024)S(1)}, f32[1536]{0:T(1024)S(1)}, f32[128]{0:T(128)S(1)}, bf16[128,1536]{1,0:T(8,128)(2,1)}, /*index=5*/f32[128,1536]{1,0:T(8,128)S(1)}) fusion(f32[144,1536]{1,0:T(8,128)} %maximum_convert_fusion, f32[1536]{0:T(1024)S(1)} %get-tuple-element.82, f32[1536]{0:T(1024)} %get-tuple-element.83, ...), kind=kOutput, calls=%fused_computation.34 | convolution fusion | flops 1114172800 | bytes 12947968 | tf_op jit(solution)/shard_map/dot_general | solution.py:121
  106.4 59.2 %psum.7 = f32[3,1536]{1,0:T(4,128)S(1)} all-reduce(f32[3,1536]{1,0:T(4,128)S(1)} %pad_maximum_fusion), channel_id=1, replica_groups=mesh['groups'=2,'seq'=16] {'seq'}, use_global_device_ids=true, to_apply=%region_8.9 | all-reduce | flops 4608 | bytes 36864 | tf_op jit(solution)/shard_map/psum | solution.py:101
  166.2 2.6 copy.21
  168.7 89.4 %while.15 = (s32[]{:T(128)}, f32[1024]{0:T(1024)S(1)}, f32[1024]{0:T(1024)S(1)}, f32[1024,192]{0,1:T(8,128)}, bf16[16,128,320]{2,1,0:T(8,128)(2,1)}, /*index=5*/bf16[1024,128]{1,0:T(8,128)(2,1)S(1)}, s32[]{:T(128)}, s32[]{:T(128)}) while((s32[]{:T(128)}, f32[1024]{0:T(1024)S(1)}, f32[1024]{0:T(1024)S(1)}, f32[1024,192]{0,1:T(8,128)}, ...), condition=%wide.region_4.5_spmd.clone, body=%wide.region_1.4_spmd.clone.sunk | while | flops 85267456 | bytes 3735653 | solution.py:72
  177.2 2.5 convolution_add_fusion.3
  182.8 2.5 convolution_add_fusion.3
  188.4 2.5 convolution_add_fusion.3
  194.0 2.5 convolution_add_fusion.3
  199.6 2.5 convolution_add_fusion.3
  205.2 2.5 convolution_add_fusion.3
  210.8 2.5 convolution_add_fusion.3
  216.4 2.5 convolution_add_fusion.3
  222.0 2.5 convolution_add_fusion.3
  227.6 2.5 convolution_add_fusion.3
  233.2 2.5 convolution_add_fusion.3
  238.8 2.5 convolution_add_fusion.3
  244.4 2.5 convolution_add_fusion.3
  250.0 2.5 convolution_add_fusion.3
  261.8 4.1 %fusion.8 = bf16[128,1536]{1,0:T(8,128)(2,1)} fusion(f32[128,1536]{1,0:T(8,128)} %copy-done.1, bf16[128,1536]{1,0:T(8,128)(2,1)S(1)} %convert_element_type.46, bf16[1536,1536]{1,0:T(8,128)(2,1)} %param.18), kind=kOutput, calls=%fused_computation.19 | convolution fusion | flops 604372992 | bytes 6291456 | tf_op jit(solution)/shard_map/dot_general | solution.py:77
  (144 shorter events, 80.2 us)
Async XLA Ops:
  7.2 95.6 %copy-start = (bf16[1536,1024]{1,0:T(8,128)(2,1)S(1)}, bf16[1536,1024]{1,0:T(8,128)(2,1)}, u32[]{:S(2)}) copy-start(bf16[1536,1024]{1,0:T(8,128)(2,1)} %param.16) | copy-start | bytes 9437188
  7.2 86.1 %all-gather.4.cloned.1.call-start = ((), (), s32[]{:S(2)}) async-start(), calls=%async_computation.1 | async-start | bytes 9191424 | tf_op jit(solution)/shard_map/all_gather | solution.py:123
  9.6 45.3 %all-to-all-start = ((bf16[16,128,12]{1,2,0:T(8,128)(2,1)}), bf16[16,128,12]{1,2,0:T(8,128)(2,1)S(1)}, u32[]{:S(2)}, u32[]{:S(2)}) async-start(bf16[16,128,12]{1,2,0:T(8,128)(2,1)} %copy.20), calls=%async_computation | async-start | bytes 131072 | tf_op jit(solution)/shard_map/all_to_all | solution.py:84
  17.0 149.2 %all-gather.6.cloned.1.call-start = ((), (), s32[]{:S(2)}) async-start(), calls=%async_computation.2 | async-start | bytes 1392640 | tf_op jit(solution)/shard_map/all_gather | solution.py:66
  57.7 7.7 %collective-permute-start = (bf16[8,1536]{1,0:T(8,128)(2,1)}, bf16[8,1536]{1,0:T(8,128)(2,1)}, u32[]{:S(2)}, u32[]{:S(2)}) collective-permute-start(bf16[8,1536]{1,0:T(8,128)(2,1)} %get-tuple-element.101), channel_id=1, source_target_pairs={{0,1},{1,2},{2,3},{3,4},{4,5},{5,6},{6,7},{7,8},{8,9},{9,10},{10,1... | collective-permute-start | bytes 73736 | tf_op jit(solution)/shard_map/ppermute | solution.py:21
  60.5 4.9 %collective-permute-start.1 = (bf16[8,1536]{1,0:T(8,128)(2,1)}, bf16[8,1536]{1,0:T(8,128)(2,1)}, u32[]{:S(2)}, u32[]{:S(2)}) collective-permute-start(bf16[8,1536]{1,0:T(8,128)(2,1)} %get-tuple-element.102), channel_id=1, source_target_pairs={{1,0},{2,1},{3,2},{4,3},{5,4},{6,5},{7,6},{8,7},{9,8},{10,9},{11,1... | collective-permute-start | bytes 73736 | tf_op jit(solution)/shard_map/ppermute | solution.py:23
  93.3 8.3 %copy-start.2 = (bf16[1536,320]{0,1:T(8,128)(2,1)S(1)}, bf16[1536,320]{0,1:T(8,128)(2,1)}, u32[]{:S(2)}) copy-start(bf16[1536,320]{0,1:T(8,128)(2,1)} %param.17) | copy-start | bytes 2949124
  93.3 8.3 %copy-start.3 = (f32[1536]{0:T(1024)S(1)}, f32[1536]{0:T(1024)}, u32[]{:S(2)}) copy-start(f32[1536]{0:T(1024)} %param.15) | copy-start | bytes 18436
  100.7 0.9 copy-start.1
Sparse Core Ops, SparseCore 0:
  10.3 82.9 all-gather.3
  102.9 36.2 all-gather.5
where the time goes:
time: 275 us; the launch traced here: 273 us
  blocking collectives  89.3 us (32%)
  matrix products  72.9 us (27%)
  local copies, waits for them, and re-layouts  33.7 us (12%)
  waiting for transfers between devices  26.8 us (10%)
  other arithmetic  24.2 us (9%)
  between operations  14.2 us (5%)
  starting transfers between devices  11.6 us (4%)
    psum x1, blocking collectives, decoder_back(): summed = lax.psum(jnp.stack(tap_terms, axis=0), 'seq')  59.2 us
    dot_general x16, matrix products, block_update(): jnp.dot(expw.astype(jnp.bfloat16), key_block[:, QK:], preferred_element_t...  39.6 us
    all_gather x1, blocking collectives, decoder_back(): every_row = lax.all_gather(track_weight, 'seq', axis=0, tiled=True)  30.1 us
    all_gather x1, waiting for transfers between devices, shards(): lax.all_gather(enc_weight, 'seq', axis=0, tiled=True)  26.1 us
    reduce_sum x16, other arithmetic, block_update(): running_sum = running_sum * shrink + jnp.sum(expw, axis=1)  18.2 us
    dot_general x16, matrix products, block_update(): lax.dot_general(query_rows, key_block[:, :QK], (((1,), (1,)), ((), ())),...  16.7 us
    squeeze x16, local copies, waits for them, and re-layouts, attention(): lax.scan(step_fn, carry, piece.reshape(count // 128, 128, piece.shape[1]))  14.4 us
    dot_general x1, matrix products, shards(): jnp.dot(patches, lax.all_gather(enc_weight, 'seq', axis=0, tiled=True), p...  7.46 us
  transfers between devices with their start and end apart: 5, of which 1 were waited for; matrix products, arithmetic and copies ran while one was open for 8% of the time, Pallas kernels for 0%

commit v1 on v0

--- a/solution.py
+++ b/solution.py
@@ -98,7 +98,7 @@
         convback = convback + dec_weight[shift_amount][None, :] * shifted_rows
         tap_terms.append(jnp.sum(skip_act * shifted_rows, axis=0))
     skip_grad = pullback(convback)[0].astype(jnp.bfloat16)
-    summed = lax.psum(jnp.stack(tap_terms, axis=0), "seq")
+    summed = jnp.sum(lax.all_gather(jnp.stack(tap_terms, axis=0), "seq"), axis=0)
     dec_weight_grad = summed / jnp.float32(math.sqrt(token_rows * lax.axis_size("seq")))
     return (skip_grad, dec_weight_grad)
 

time: 275 us -> 249 us (0.905)
  blocking collectives: 89.3 us -> 52 us
  waiting for transfers between devices: 26.8 us -> 36.2 us
    psum x1 -> x0, blocking collectives: 59.2 us -> none  [decoder_back(): summed = lax.psum(jnp.stack(tap_terms, axis=0), 'seq')]
    all_gather x0 -> x1, blocking collectives: none -> 21.9 us  [decoder_back(): lax.all_gather(jnp.stack(tap_terms, axis=0), 'seq')]
    all_gather x1, waiting for transfers between devices: 0.01 us -> 9.47 us  [attention(): piece = lax.all_gather(keyval, 'seq', axis=0, tiled=True)]
  transfers between devices with their start and end apart: 5 -> 5, of which waited for: 1 -> 2; matrix products, arithmetic and copies ran while one was open for 8% -> 9% of each run, Pallas kernels for 0% -> 0%
where the time goes in v1:
time: 249 us; the launch traced here: 246 us
  matrix products  73 us (29%)
  blocking collectives  52 us (21%)
  waiting for transfers between devices  36.2 us (15%)
  local copies, waits for them, and re-layouts  33.7 us (14%)
  other arithmetic  25.2 us (10%)
  between operations  14.2 us (6%)
  starting transfers between devices  11.6 us (5%)
    dot_general x16, matrix products, block_update(): jnp.dot(expw.astype(jnp.bfloat16), key_block[:, QK:], preferred_element_t...  39.7 us
    all_gather x1, blocking collectives, decoder_back(): every_row = lax.all_gather(track_weight, 'seq', axis=0, tiled=True)  30.1 us
    all_gather x1, waiting for transfers between devices, shards(): lax.all_gather(enc_weight, 'seq', axis=0, tiled=True)  26.1 us
    all_gather x1, blocking collectives, decoder_back(): lax.all_gather(jnp.stack(tap_terms, axis=0), 'seq')  21.9 us
    reduce_sum x16, other arithmetic, block_update(): running_sum = running_sum * shrink + jnp.sum(expw, axis=1)  18.2 us
    dot_general x16, matrix products, block_update(): lax.dot_general(query_rows, key_block[:, :QK], (((1,), (1,)), ((), ())),...  16.7 us
    squeeze x16, local copies, waits for them, and re-layouts, attention(): lax.scan(step_fn, carry, piece.reshape(count // 128, 128, piece.shape[1]))  14.4 us
    all_gather x1, waiting for transfers between devices, attention(): piece = lax.all_gather(keyval, 'seq', axis=0, tiled=True)  9.47 us
  transfers between devices with their start and end apart: 5, of which 2 were waited for; matrix products, arithmetic and copies ran while one was open for 9% of the time, Pallas kernels for 0%

profile of v1, /device:TPU:0, one launch (start us, length us, event | category | flops | bytes accessed | tf_op | source)
XLA Modules:
  0.0 246.1 jit_solution(6367389038292693644)
XLA Ops:
  9.6 7.4 %all-to-all-start = ((bf16[16,128,12]{1,2,0:T(8,128)(2,1)}), bf16[16,128,12]{1,2,0:T(8,128)(2,1)S(1)}, u32[]{:S(2)}, u32[]{:S(2)}) async-start(bf16[16,128,12]{1,2,0:T(8,128)(2,1)} %copy.20), calls=%async_computation | async-start | bytes 131072 | tf_op jit(solution)/shard_map/all_to_all | solution.py:84
  17.1 30.1 %all-gather.1 = bf16[16,12,1536]{2,1,0:T(8,128)(2,1)} all-gather(bf16[1,12,1536]{2,1,0:T(8,128)(2,1)} %bitcast.30), channel_id=1, replica_groups=mesh['groups'=2,'seq'=16] {'seq'}, dimensions={0}, use_global_device_ids=true | all-gather | bytes 626688 | tf_op jit(solution)/shard_map/all_gather | solution.py:86
  51.3 3.6 %gather_fusion = bf16[192,1536]{1,0:T(8,128)(2,1)} fusion(bf16[192,1536]{1,0:T(8,128)(2,1)} %reshape.52, s32[1024]{0:T(1024)S(1)} %pad_clamp_fusion), kind=kCustom, calls=%fused_computation | custom fusion | bytes 1180416 | tf_op jit(solution)/shard_map/jit(_take)/gather | solution.py:87
  57.7 2.8 %collective-permute-start = (bf16[8,1536]{1,0:T(8,128)(2,1)}, bf16[8,1536]{1,0:T(8,128)(2,1)}, u32[]{:S(2)}, u32[]{:S(2)}) collective-permute-start(bf16[8,1536]{1,0:T(8,128)(2,1)} %get-tuple-element.101), channel_id=1, source_target_pairs={{0,1},{1,2},{2,3},{3,4},{4,5},{5,6},{6,7},{7,8},{8,9},{9,10},{10,1... | collective-permute-start | bytes 73736 | tf_op jit(solution)/shard_map/ppermute | solution.py:21
  67.2 26.1 %all-gather.6.cloned.1.call-done = bf16[2816,1536]{1,0:T(8,128)(2,1)} async-done(((bf16[176,1536]{1,0:T(8,128)(2,1)}), bf16[2816,1536]{1,0:T(8,128)(2,1)}) %all-gather.6.cloned.1.call-update) | async-done | bytes 8650768 | tf_op jit(solution)/shard_map/all_gather | solution.py:123
  93.3 7.5 %multiply_reduce_fusion.3 = (f32[1536]{0:T(1024)S(1)}, f32[1536]{0:T(1024)S(1)}, f32[1536]{0:T(1024)S(1)}, f32[128]{0:T(128)S(1)}, bf16[128,1536]{1,0:T(8,128)(2,1)}, /*index=5*/f32[128,1536]{1,0:T(8,128)S(1)}) fusion(f32[144,1536]{1,0:T(8,128)} %maximum_convert_fusion, f32[1536]{0:T(1024)S(1)} %get-tuple-element.82, f32[1536]{0:T(1024)} %get-tuple-element.83, ...), kind=kOutput, calls=%fused_computation.34 | convolution fusion | flops 1114172800 | bytes 12947968 | tf_op jit(solution)/shard_map/dot_general | solution.py:121
  106.4 21.9 %all-gather.2 = f32[16,3,1536]{2,1,0:T(4,128)} all-gather(f32[1,3,1536]{2,1,0:T(4,128)S(1)} %maximum_bitcast_fusion), channel_id=2, replica_groups=mesh['groups'=2,'seq'=16] {'seq'}, dimensions={0}, use_global_device_ids=true | all-gather | bytes 313344 | tf_op jit(solution)/shard_map/all_gather | solution.py:101
  130.0 9.5 %all-gather.8.cloned.1.call-done = bf16[2048,320]{0,1:T(8,128)(2,1)} async-done(((bf16[128,320]{0,1:T(8,128)(2,1)}), bf16[2048,320]{0,1:T(8,128)(2,1)}) %all-gather.8.cloned.1.call-update) | async-done | bytes 1310736 | tf_op jit(solution)/shard_map/all_gather | solution.py:66
  139.5 2.6 %copy.21 = bf16[2048,320]{1,0:T(8,128)(2,1)} copy(bf16[2048,320]{0,1:T(8,128)(2,1)} %all-gather.8.cloned.1.call-done) | data formatting | bytes 2621440
  142.0 89.4 %while.15 = (s32[]{:T(128)}, f32[1024]{0:T(1024)S(1)}, f32[1024]{0:T(1024)S(1)}, f32[1024,192]{0,1:T(8,128)}, bf16[16,128,320]{2,1,0:T(8,128)(2,1)}, /*index=5*/bf16[1024,128]{1,0:T(8,128)(2,1)S(1)}, s32[]{:T(128)}, s32[]{:T(128)}) while((s32[]{:T(128)}, f32[1024]{0:T(1024)S(1)}, f32[1024]{0:T(1024)S(1)}, f32[1024,192]{0,1:T(8,128)}, ...), condition=%wide.region_4.5_spmd.clone, body=%wide.region_1.4_spmd.clone.sunk | while | flops 85267456 | bytes 3735653 | solution.py:72
  150.5 2.5 %convolution_add_fusion.3 = f32[1024,192]{0,1:T(8,128)} fusion(f32[1024,192]{0,1:T(8,128)} %get-tuple-element.160, f32[1024]{0:T(1024)S(1)} %get-tuple-element.148, pred[]{:T(512)S(6)} %compare.3, f32[128,1024]{1,0:T(8,128)} %get-tuple-element.146, f32[1024]{0:T(1024)S(1)} %select_maximum_fusion.2, bf16[128,320]{1,0:T(8,128)(2,1)S(1)} %dynamic-slice_bitcast_fusion.2), kind=kOutput, calls=%fused_computation.1.clone.1 | convolution fusion | flops 51183616 | bytes 2170881 | tf_op jit(solution)/shard_map/while/body/eval_jaxpr/dot_general | solution.py:55
  156.1 2.5 %convolution_add_fusion.3 = f32[1024,192]{0,1:T(8,128)} fusion(f32[1024,192]{0,1:T(8,128)} %get-tuple-element.160, f32[1024]{0:T(1024)S(1)} %get-tuple-element.148, pred[]{:T(512)S(6)} %compare.3, f32[128,1024]{1,0:T(8,128)} %get-tuple-element.146, f32[1024]{0:T(1024)S(1)} %select_maximum_fusion.2, bf16[128,320]{1,0:T(8,128)(2,1)S(1)} %dynamic-slice_bitcast_fusion.2), kind=kOutput, calls=%fused_computation.1.clone.1 | convolution fusion | flops 51183616 | bytes 2170881 | tf_op jit(solution)/shard_map/while/body/eval_jaxpr/dot_general | solution.py:55
  161.7 2.5 %convolution_add_fusion.3 = f32[1024,192]{0,1:T(8,128)} fusion(f32[1024,192]{0,1:T(8,128)} %get-tuple-element.160, f32[1024]{0:T(1024)S(1)} %get-tuple-element.148, pred[]{:T(512)S(6)} %compare.3, f32[128,1024]{1,0:T(8,128)} %get-tuple-element.146, f32[1024]{0:T(1024)S(1)} %select_maximum_fusion.2, bf16[128,320]{1,0:T(8,128)(2,1)S(1)} %dynamic-slice_bitcast_fusion.2), kind=kOutput, calls=%fused_computation.1.clone.1 | convolution fusion | flops 51183616 | bytes 2170881 | tf_op jit(solution)/shard_map/while/body/eval_jaxpr/dot_general | solution.py:55
  167.3 2.5 %convolution_add_fusion.3 = f32[1024,192]{0,1:T(8,128)} fusion(f32[1024,192]{0,1:T(8,128)} %get-tuple-element.160, f32[1024]{0:T(1024)S(1)} %get-tuple-element.148, pred[]{:T(512)S(6)} %compare.3, f32[128,1024]{1,0:T(8,128)} %get-tuple-element.146, f32[1024]{0:T(1024)S(1)} %select_maximum_fusion.2, bf16[128,320]{1,0:T(8,128)(2,1)S(1)} %dynamic-slice_bitcast_fusion.2), kind=kOutput, calls=%fused_computation.1.clone.1 | convolution fusion | flops 51183616 | bytes 2170881 | tf_op jit(solution)/shard_map/while/body/eval_jaxpr/dot_general | solution.py:55
  172.9 2.5 %convolution_add_fusion.3 = f32[1024,192]{0,1:T(8,128)} fusion(f32[1024,192]{0,1:T(8,128)} %get-tuple-element.160, f32[1024]{0:T(1024)S(1)} %get-tuple-element.148, pred[]{:T(512)S(6)} %compare.3, f32[128,1024]{1,0:T(8,128)} %get-tuple-element.146, f32[1024]{0:T(1024)S(1)} %select_maximum_fusion.2, bf16[128,320]{1,0:T(8,128)(2,1)S(1)} %dynamic-slice_bitcast_fusion.2), kind=kOutput, calls=%fused_computation.1.clone.1 | convolution fusion | flops 51183616 | bytes 2170881 | tf_op jit(solution)/shard_map/while/body/eval_jaxpr/dot_general | solution.py:55
  178.5 2.5 %convolution_add_fusion.3 = f32[1024,192]{0,1:T(8,128)} fusion(f32[1024,192]{0,1:T(8,128)} %get-tuple-element.160, f32[1024]{0:T(1024)S(1)} %get-tuple-element.148, pred[]{:T(512)S(6)} %compare.3, f32[128,1024]{1,0:T(8,128)} %get-tuple-element.146, f32[1024]{0:T(1024)S(1)} %select_maximum_fusion.2, bf16[128,320]{1,0:T(8,128)(2,1)S(1)} %dynamic-slice_bitcast_fusion.2), kind=kOutput, calls=%fused_computation.1.clone.1 | convolution fusion | flops 51183616 | bytes 2170881 | tf_op jit(solution)/shard_map/while/body/eval_jaxpr/dot_general | solution.py:55
  184.1 2.5 %convolution_add_fusion.3 = f32[1024,192]{0,1:T(8,128)} fusion(f32[1024,192]{0,1:T(8,128)} %get-tuple-element.160, f32[1024]{0:T(1024)S(1)} %get-tuple-element.148, pred[]{:T(512)S(6)} %compare.3, f32[128,1024]{1,0:T(8,128)} %get-tuple-element.146, f32[1024]{0:T(1024)S(1)} %select_maximum_fusion.2, bf16[128,320]{1,0:T(8,128)(2,1)S(1)} %dynamic-slice_bitcast_fusion.2), kind=kOutput, calls=%fused_computation.1.clone.1 | convolution fusion | flops 51183616 | bytes 2170881 | tf_op jit(solution)/shard_map/while/body/eval_jaxpr/dot_general | solution.py:55
  189.7 2.5 %convolution_add_fusion.3 = f32[1024,192]{0,1:T(8,128)} fusion(f32[1024,192]{0,1:T(8,128)} %get-tuple-element.160, f32[1024]{0:T(1024)S(1)} %get-tuple-element.148, pred[]{:T(512)S(6)} %compare.3, f32[128,1024]{1,0:T(8,128)} %get-tuple-element.146, f32[1024]{0:T(1024)S(1)} %select_maximum_fusion.2, bf16[128,320]{1,0:T(8,128)(2,1)S(1)} %dynamic-slice_bitcast_fusion.2), kind=kOutput, calls=%fused_computation.1.clone.1 | convolution fusion | flops 51183616 | bytes 2170881 | tf_op jit(solution)/shard_map/while/body/eval_jaxpr/dot_general | solution.py:55
  195.3 2.5 %convolution_add_fusion.3 = f32[1024,192]{0,1:T(8,128)} fusion(f32[1024,192]{0,1:T(8,128)} %get-tuple-element.160, f32[1024]{0:T(1024)S(1)} %get-tuple-element.148, pred[]{:T(512)S(6)} %compare.3, f32[128,1024]{1,0:T(8,128)} %get-tuple-element.146, f32[1024]{0:T(1024)S(1)} %select_maximum_fusion.2, bf16[128,320]{1,0:T(8,128)(2,1)S(1)} %dynamic-slice_bitcast_fusion.2), kind=kOutput, calls=%fused_computation.1.clone.1 | convolution fusion | flops 51183616 | bytes 2170881 | tf_op jit(solution)/shard_map/while/body/eval_jaxpr/dot_general | solution.py:55
  200.9 2.5 %convolution_add_fusion.3 = f32[1024,192]{0,1:T(8,128)} fusion(f32[1024,192]{0,1:T(8,128)} %get-tuple-element.160, f32[1024]{0:T(1024)S(1)} %get-tuple-element.148, pred[]{:T(512)S(6)} %compare.3, f32[128,1024]{1,0:T(8,128)} %get-tuple-element.146, f32[1024]{0:T(1024)S(1)} %select_maximum_fusion.2, bf16[128,320]{1,0:T(8,128)(2,1)S(1)} %dynamic-slice_bitcast_fusion.2), kind=kOutput, calls=%fused_computation.1.clone.1 | convolution fusion | flops 51183616 | bytes 2170881 | tf_op jit(solution)/shard_map/while/body/eval_jaxpr/dot_general | solution.py:55
  206.5 2.5 %convolution_add_fusion.3 = f32[1024,192]{0,1:T(8,128)} fusion(f32[1024,192]{0,1:T(8,128)} %get-tuple-element.160, f32[1024]{0:T(1024)S(1)} %get-tuple-element.148, pred[]{:T(512)S(6)} %compare.3, f32[128,1024]{1,0:T(8,128)} %get-tuple-element.146, f32[1024]{0:T(1024)S(1)} %select_maximum_fusion.2, bf16[128,320]{1,0:T(8,128)(2,1)S(1)} %dynamic-slice_bitcast_fusion.2), kind=kOutput, calls=%fused_computation.1.clone.1 | convolution fusion | flops 51183616 | bytes 2170881 | tf_op jit(solution)/shard_map/while/body/eval_jaxpr/dot_general | solution.py:55
  217.7 2.5 %convolution_add_fusion.3 = f32[1024,192]{0,1:T(8,128)} fusion(f32[1024,192]{0,1:T(8,128)} %get-tuple-element.160, f32[1024]{0:T(1024)S(1)} %get-tuple-element.148, pred[]{:T(512)S(6)} %compare.3, f32[128,1024]{1,0:T(8,128)} %get-tuple-element.146, f32[1024]{0:T(1024)S(1)} %select_maximum_fusion.2, bf16[128,320]{1,0:T(8,128)(2,1)S(1)} %dynamic-slice_bitcast_fusion.2), kind=kOutput, calls=%fused_computation.1.clone.1 | convolution fusion | flops 51183616 | bytes 2170881 | tf_op jit(solution)/shard_map/while/body/eval_jaxpr/dot_general | solution.py:55
  228.9 2.5 %convolution_add_fusion.3 = f32[1024,192]{0,1:T(8,128)} fusion(f32[1024,192]{0,1:T(8,128)} %get-tuple-element.160, f32[1024]{0:T(1024)S(1)} %get-tuple-element.148, pred[]{:T(512)S(6)} %compare.3, f32[128,1024]{1,0:T(8,128)} %get-tuple-element.146, f32[1024]{0:T(1024)S(1)} %select_maximum_fusion.2, bf16[128,320]{1,0:T(8,128)(2,1)S(1)} %dynamic-slice_bitcast_fusion.2), kind=kOutput, calls=%fused_computation.1.clone.1 | convolution fusion | flops 51183616 | bytes 2170881 | tf_op jit(solution)/shard_map/while/body/eval_jaxpr/dot_general | solution.py:55
  235.1 4.1 %fusion.8 = bf16[128,1536]{1,0:T(8,128)(2,1)} fusion(f32[128,1536]{1,0:T(8,128)} %copy-done.1, bf16[128,1536]{1,0:T(8,128)(2,1)S(1)} %convert_element_type.46, bf16[1536,1536]{1,0:T(8,128)(2,1)} %param.18), kind=kOutput, calls=%fused_computation.19 | convolution fusion | flops 604372992 | bytes 6291456 | tf_op jit(solution)/shard_map/dot_general | solution.py:77
  (145 shorter events, 83.9 us)
Async XLA Ops:
  7.2 95.6 %copy-start = (bf16[1536,1024]{1,0:T(8,128)(2,1)S(1)}, bf16[1536,1024]{1,0:T(8,128)(2,1)}, u32[]{:S(2)}) copy-start(bf16[1536,1024]{1,0:T(8,128)(2,1)} %param.16) | copy-start | bytes 9437188
  7.2 86.1 %all-gather.6.cloned.1.call-start = ((), (), s32[]{:S(2)}) async-start(), calls=%async_computation.1 | async-start | bytes 9191424 | tf_op jit(solution)/shard_map/all_gather | solution.py:123
  9.6 45.3 %all-to-all-start = ((bf16[16,128,12]{1,2,0:T(8,128)(2,1)}), bf16[16,128,12]{1,2,0:T(8,128)(2,1)S(1)}, u32[]{:S(2)}, u32[]{:S(2)}) async-start(bf16[16,128,12]{1,2,0:T(8,128)(2,1)} %copy.20), calls=%async_computation | async-start | bytes 131072 | tf_op jit(solution)/shard_map/all_to_all | solution.py:84
  17.0 122.4 %all-gather.8.cloned.1.call-start = ((), (), s32[]{:S(2)}) async-start(), calls=%async_computation.2 | async-start | bytes 1392640 | tf_op jit(solution)/shard_map/all_gather | solution.py:66
  57.7 7.7 %collective-permute-start = (bf16[8,1536]{1,0:T(8,128)(2,1)}, bf16[8,1536]{1,0:T(8,128)(2,1)}, u32[]{:S(2)}, u32[]{:S(2)}) collective-permute-start(bf16[8,1536]{1,0:T(8,128)(2,1)} %get-tuple-element.101), channel_id=1, source_target_pairs={{0,1},{1,2},{2,3},{3,4},{4,5},{5,6},{6,7},{7,8},{8,9},{9,10},{10,1... | collective-permute-start | bytes 73736 | tf_op jit(solution)/shard_map/ppermute | solution.py:21
  60.5 4.9 %collective-permute-start.1 = (bf16[8,1536]{1,0:T(8,128)(2,1)}, bf16[8,1536]{1,0:T(8,128)(2,1)}, u32[]{:S(2)}, u32[]{:S(2)}) collective-permute-start(bf16[8,1536]{1,0:T(8,128)(2,1)} %get-tuple-element.102), channel_id=1, source_target_pairs={{1,0},{2,1},{3,2},{4,3},{5,4},{6,5},{7,6},{8,7},{9,8},{10,9},{11,1... | collective-permute-start | bytes 73736 | tf_op jit(solution)/shard_map/ppermute | solution.py:23
  93.3 8.3 %copy-start.2 = (bf16[1536,320]{0,1:T(8,128)(2,1)S(1)}, bf16[1536,320]{0,1:T(8,128)(2,1)}, u32[]{:S(2)}) copy-start(bf16[1536,320]{0,1:T(8,128)(2,1)} %param.17) | copy-start | bytes 2949124
  93.3 8.3 %copy-start.3 = (f32[1536]{0:T(1024)S(1)}, f32[1536]{0:T(1024)}, u32[]{:S(2)}) copy-start(f32[1536]{0:T(1024)} %param.15) | copy-start | bytes 18436
  100.7 0.9 copy-start.1
Sparse Core Ops, SparseCore 0:
  10.3 82.9 all-gather.5
  102.9 36.5 all-gather.7
